TPU v7x, 128 devices: a whole 4x4x4 slice. The times are simulated.
128 devices in a mesh: tok: 8 (over y, core), head: 16 (over x, z).
Axes of the slice: x: 4, y: 4, z: 4, core: 2. Of those that a mesh axis runs over, the one named last changes fastest.
Arguments:
- hidden_states: bfloat16 [5120, 6144], P('tok', 'head'), may hold values from -6 to 6
- norm_gain: float32 [6144], replicated, may hold values from 0.5 to 1.5
- norm_bias: float32 [6144], replicated, may hold values from -2 to 2
- qkv_weight: bfloat16 [6144, 18432], P('tok', 'head'), may hold values from -0.125 to 0.125
- qkv_bias: bfloat16 [18432], P('head'), may hold values from -2 to 2
- dense_weight: bfloat16 [6144, 6144], P('head'), may hold values from -0.21875 to 0.21875
- dense_bias: bfloat16 [6144], P('head'), may hold values from -2 to 2
- prefix_keys: bfloat16 [16, 2048, 6144], P('tok', None, 'head'), may hold values from -70 to 70
- prefix_values: bfloat16 [16, 2048, 6144], P('tok', None, 'head'), may hold values from -10 to 10
- suffix_len: int32 [8, 16], P('tok'), may hold values from 1 to 120, as said below
- request_order: int32 [8, 16], P('tok'), may hold values from 0 to 15, each once within a row
- group_slot: int32 [16], replicated, may hold values from 0 to 15, each once
Outputs:
- layer_out: bfloat16 [5120, 6144], P('tok', 'head')
Inputs may be any that keep to these rules, and one draw needn't show every extreme that they name: `suffix_len`: each row sums to 640; one group, the same in every row, has exactly 120 in every row. `request_order`: each row names every group once. `group_slot`: each slot holds one group.
All inputs are finite; a program needn't handle non-finite values.
Results may differ from a plain program's by a relative error of at most 0.007.
The roundings to bfloat16 on the way count: a program that leaves them out, or rounds other values in their place, can miss the bound.
Values may be sent and summed in bfloat16 or wider, within the bound.
A program may use at most 128 MiB of HBM per device.

v0:
```python
import jax
import jax.numpy as jnp
from jax import lax
from jax.sharding import PartitionSpec as P

HS = 96


def layer_norm(values_in, gain, shift):
    widened = values_in.astype(jnp.float32)
    center = jnp.mean(widened, axis=-1, keepdims=True)
    spread = jnp.mean(jnp.square(widened - center), axis=-1, keepdims=True)
    return ((widened - center) * lax.rsqrt(spread + 1e-05) * gain + shift).astype(jnp.bfloat16)


def shard_layout(lengths, ordering, row_count):
    group_count = lengths.shape[0]
    labels = jnp.arange(group_count, dtype=jnp.int32)
    chosen = (ordering[:, None] == labels[None, :]).astype(jnp.int32)
    ranking = jnp.sum(labels[:, None] * chosen, axis=0)
    earlier = (ranking[None, :] < ranking[:, None]).astype(jnp.int32)
    starts = jnp.sum(earlier * lengths[None, :], axis=1)
    places = jnp.arange(row_count, dtype=jnp.int32)
    member = (
        (places[:, None] >= starts[None, :]) & (places[:, None] < (starts + lengths)[None, :])
    ).astype(jnp.int32)
    group_of = jnp.sum(member * labels[None, :], axis=1)
    within = places - jnp.sum(member * starts[None, :], axis=1)
    return (starts, member, group_of, within)


def rotary(tensor, positions, rot_dims):
    half_dims = rot_dims // 2
    inverse = 10000.0 ** (-(jnp.arange(half_dims, dtype=jnp.float32) * 2.0) / rot_dims)
    angles = positions.astype(jnp.float32)[:, None] * inverse[None, :]
    cosine = jnp.cos(angles)[:, None, :]
    sine_part = jnp.sin(angles)[:, None, :]
    lower_half = tensor[..., :half_dims]
    upper_half = tensor[..., half_dims:rot_dims]
    return jnp.concatenate(
        [
            lower_half * cosine - upper_half * sine_part,
            upper_half * cosine + lower_half * sine_part,
            tensor[..., rot_dims:],
        ],
        axis=-1,
    )


def local_suffix(queries, keys_new, values_new, group_of):
    scaling = HS ** (-0.5)
    scores = (
        jnp.einsum("ihd,jhd->hij", queries, keys_new, preferred_element_type=jnp.float32) * scaling
    )
    places = jnp.arange(queries.shape[0], dtype=jnp.int32)
    allowed = (group_of[:, None] == group_of[None, :]) & (places[None, :] <= places[:, None])
    masked = jnp.where(allowed[None], scores, -jnp.inf)
    row_peak = jnp.max(masked, axis=-1)
    weights = jnp.exp(masked - row_peak[..., None])
    row_mass = jnp.sum(weights, axis=-1)
    blended = (
        jnp.einsum(
            "hij,jhd->ihd",
            weights.astype(jnp.bfloat16),
            values_new,
            preferred_element_type=jnp.float32,
        )
        / jnp.transpose(row_mass)[..., None]
    )
    return (jnp.transpose(row_peak), jnp.transpose(row_mass), blended)


def prefix_slot(operands):
    queries_in, keys_in, values_in = operands
    row_total = queries_in.shape[0]
    local_width = queries_in.shape[1]
    local_heads = local_width // HS
    prefix_length = keys_in.shape[0]
    query_heads = queries_in.reshape(row_total, local_heads, HS)
    key_heads = keys_in.reshape(prefix_length, local_heads, HS)
    value_heads = values_in.reshape(prefix_length, local_heads, HS)
    scores = jnp.einsum(
        "rhd,phd->hrp", query_heads, key_heads, preferred_element_type=jnp.float32
    ) * HS ** (-0.5)
    row_peak = jnp.max(scores, axis=-1)
    weights = jnp.exp(scores - row_peak[..., None])
    row_mass = jnp.sum(weights, axis=-1)
    blended = (
        jnp.einsum(
            "hrp,phd->rhd",
            weights.astype(jnp.bfloat16),
            value_heads,
            preferred_element_type=jnp.float32,
        )
        / jnp.transpose(row_mass)[..., None]
    )
    return (
        blended.reshape(row_total, local_width),
        jnp.transpose(row_peak),
        jnp.transpose(row_mass),
    )


def on_device(
    hidden_states,
    norm_gain,
    norm_bias,
    qkv_weight,
    qkv_bias,
    dense_weight,
    dense_bias,
    prefix_keys,
    prefix_values,
    suffix_len,
    request_order,
    group_slot,
):
    tok_rows = hidden_states.shape[0]
    slot_local = prefix_keys.shape[0]
    prefix_length = prefix_keys.shape[1]
    local_width = prefix_keys.shape[2]
    local_heads = local_width // HS
    group_count = slot_local * lax.axis_size("tok")
    capacity = 3 * tok_rows // group_count
    full_rows = lax.all_gather(hidden_states, "head", axis=1, tiled=True)
    normed = layer_norm(full_rows, norm_gain, norm_bias)
    projected = jnp.dot(
        normed,
        lax.all_gather(qkv_weight, "tok", axis=0, tiled=True),
        preferred_element_type=jnp.float32,
    )
    projected = (projected + qkv_bias.astype(jnp.float32)).reshape(tok_rows, local_heads, 3, HS)
    lengths = suffix_len[0]
    starts, member, group_of, within = shard_layout(lengths, request_order[0], tok_rows)
    positions = prefix_length + within
    queries = rotary(projected[:, :, 0], positions, HS // 4).astype(jnp.bfloat16)
    keys_new = rotary(projected[:, :, 1], positions, HS // 4).astype(jnp.bfloat16)
    values_new = projected[:, :, 2].astype(jnp.bfloat16)
    suf_peak, suf_mass, suf_out = local_suffix(queries, keys_new, values_new, group_of)
    labels = jnp.arange(group_count, dtype=jnp.int32)
    slot_match = (group_slot[:, None] == labels[None, :]).astype(jnp.int32)
    slot_starts = jnp.sum(starts[:, None] * slot_match, axis=0)
    slot_lengths = jnp.sum(lengths[:, None] * slot_match, axis=0)
    cap_index = jnp.arange(capacity, dtype=jnp.int32)
    live_slot = cap_index[None, :] < slot_lengths[:, None]
    source_rows = jnp.where(live_slot, slot_starts[:, None] + cap_index[None, :], 0)
    flat_query = queries.reshape(tok_rows, local_width)
    outgoing = jnp.where(live_slot[..., None], flat_query[source_rows], jnp.zeros((), jnp.bfloat16))
    incoming = lax.all_to_all(outgoing, "tok", split_axis=0, concat_axis=1, tiled=True)
    pre_all, peak_all, mass_all = lax.map(prefix_slot, (incoming, prefix_keys, prefix_values))
    returned = (
        lax.all_to_all(pre_all, "tok", split_axis=1, concat_axis=0, tiled=True),
        lax.all_to_all(peak_all, "tok", split_axis=1, concat_axis=0, tiled=True),
        lax.all_to_all(mass_all, "tok", split_axis=1, concat_axis=0, tiled=True),
    )
    token_slot = jnp.sum(member * group_slot[None, :], axis=1)
    flat_index = token_slot * capacity + within
    pre_out = returned[0].reshape(group_count * capacity, local_heads, HS)[flat_index]
    pre_peak = returned[1].reshape(group_count * capacity, local_heads)[flat_index]
    pre_mass = returned[2].reshape(group_count * capacity, local_heads)[flat_index]
    joint_peak = jnp.maximum(pre_peak, suf_peak)
    pre_share = pre_mass * jnp.exp(pre_peak - joint_peak)
    suf_share = suf_mass * jnp.exp(suf_peak - joint_peak)
    combined = (pre_share[..., None] * pre_out + suf_share[..., None] * suf_out) / (
        pre_share + suf_share
    )[..., None]
    attention = combined.reshape(tok_rows, local_width).astype(jnp.bfloat16)
    partial_out = jnp.dot(attention, dense_weight, preferred_element_type=jnp.float32)
    summed = lax.psum_scatter(partial_out, "head", scatter_dimension=1, tiled=True)
    return (hidden_states.astype(jnp.float32) + dense_bias.astype(jnp.float32) + summed).astype(
        jnp.bfloat16
    )


def solution(mesh):
    placed = (
        P("tok", "head"),
        P(),
        P(),
        P("tok", "head"),
        P("head"),
        P("head", None),
        P("head"),
        P("tok", None, "head"),
        P("tok", None, "head"),
        P("tok", None),
        P("tok", None),
        P(),
    )
    return jax.shard_map(
        on_device, mesh=mesh, in_specs=placed, out_specs=P("tok", "head"), check_vma=False
    )
```

profile of v0, /device:TPU:0, one launch (start us, length us, event | category | flops | bytes accessed | tf_op | source)
XLA Modules:
  0.0 575.5 jit_solution(17584146502956771030)
XLA Ops:
  14.1 73.6 %all-gather.3.cloned.1.call-done = bf16[640,6144]{1,0:T(8,128)(2,1)} async-done(((bf16[640,384]{1,0:T(8,128)(2,1)}), bf16[640,6144]{1,0:T(8,128)(2,1)}) %all-gather.3.cloned.1.call-update) | async-done | bytes 7864336 | tf_op jit(solution)/shard_map/all_gather | solution.py:125
  87.8 4.5 convert_reduce_fusion
  93.3 2.2 fusion.9
  95.4 67.3 %all-gather.5.cloned.1.call-done = bf16[6144,1152]{1,0:T(8,128)(2,1)} async-done(((bf16[768,1152]{1,0:T(8,128)(2,1)}), bf16[6144,1152]{1,0:T(8,128)(2,1)}) %all-gather.5.cloned.1.call-update) | async-done | bytes 14155792 | tf_op jit(solution)/shard_map/all_gather | solution.py:129
  162.7 18.1 %fusion.22 = f32[640,1152]{1,0:T(8,128)} fusion(bf16[6144,1152]{1,0:T(8,128)(2,1)} %all-gather.5.cloned.1.call-done, bf16[640,6144]{1,0:T(8,128)(2,1)} %all-gather.3.cloned.1.call-done, f32[6144]{0:T(1024)S(1)} %copy-done.17, f32[6144]{0:T(1024)S(1)} %copy-done.18, f32[640]{0:T(1024)S(1)} %add_rsqrt_fusion, f32[640]{0:T(1024)S(1)} %broadcast_multiply_fusion.1, ...), kind=kOutput, calls=%fused_computation.34 | convolution fusion | flops 9084026880 | bytes 25028096 | tf_op jit(solution)/shard_map/dot_general | solution.py:127
  180.9 3.1 copy.119
  186.1 6.4 %gather_fusion = bf16[1920,384]{1,0:T(8,128)(2,1)S(1)} fusion(bf16[640,384]{1,0:T(8,128)(2,1)S(1)} %copy.121, s32[2048]{0:T(1024)S(1)} %pad_clamp_fusion), kind=kCustom, calls=%fused_computation | custom fusion | bytes 2956800 | tf_op jit(solution)/shard_map/gather | solution.py:148
  194.1 3.8 all-to-all-start
  197.9 20.2 %all-to-all-done = bf16[16,120,384]{2,1,0:T(8,128)(2,1)S(1)} async-done(((bf16[16,120,384]{2,1,0:T(8,128)(2,1)}), bf16[16,120,384]{2,1,0:T(8,128)(2,1)S(1)}, u32[]{:S(2)}, u32[]{:S(2)}) %all-to-all-start) | async-done | bytes 1474592 | tf_op jit(solution)/shard_map/all_to_all | solution.py:149
  219.4 158.2 %while.14 = (s32[]{:T(128)}, f32[2,960,384]{2,0,1:T(2,128)}, f32[2,960,4]{1,2,0:T(4,128)S(1)}, f32[2,960,4]{1,2,0:T(4,128)S(1)}, bf16[2,2048,384]{2,1,0:T(8,128)...) while((s32[]{:T(128)}, f32[2,960,384]{2,0,1:T(2,128)}, ...), condition=%wide.region_10.11_spmd, body=%wide.region_7.10_spmd.sunk | while | flops 3083174400 | bytes 127593616 | solution.py:150
  227.4 13.6 %multiply_reduce_fusion.2 = (f32[4,960]{1,0:T(4,128)S(1)}, f32[4,960,2048]{2,1,0:T(8,128)}) fusion(bf16[960,4,96]{0,2,1:T(8,128)(2,1)} %bitcast.96, bf16[2048,4,96]{0,2,1:T(8,128)(2,1)S(1)} %bitcast.95), kind=kOutput, calls=%fused_computation.5.clone.1 | convolution fusion | flops 1525674240 | bytes 33782784 | tf_op jit(solution)/shard_map/while/body/eval_jaxpr/rhd,phd->hrp/dot_general | solution.py:82
  241.0 13.8 %fusion.74 = f32[4,960]{1,0:T(4,128)S(1)} fusion(f32[4,960,2048]{2,1,0:T(8,128)} %get-tuple-element.176, f32[4,960]{1,0:T(4,128)S(1)} %get-tuple-element.177), kind=kLoop, calls=%fused_computation.6.clone.1 | loop fusion | flops 23589120 | bytes 31488000 | tf_op jit(solution)/shard_map/while/body/eval_jaxpr/reduce_sum | solution.py:87
  254.8 12.8 %bitcast_divide_fusion.2 = f32[960,4,96]{0,2,1:T(8,128)S(1)} fusion(bf16[2048,4,96]{0,2,1:T(8,128)(2,1)S(1)} %bitcast.97, f32[4,960,2048]{2,1,0:T(8,128)} %get-tuple-element.176, f32[4,960]{1,0:T(4,128)S(1)} %get-tuple-element.177, f32[960,4]{0,1:T(4,128)S(1)} %bitcast.113), kind=kOutput, calls=%fused_computation.9.clone.1 | convolution fusion | flops 1533911040 | bytes 34535424 | tf_op jit(solution)/shard_map/while/body/eval_jaxpr/hrp,phd->rhd/dot_general | solution.py:89
  267.6 2.3 copy.168
  269.9 28.5 %dynamic_update_slice.16 = f32[2,960,384]{2,0,1:T(2,128)} dynamic-update-slice(f32[2,960,384]{2,0,1:T(2,128)} %get-tuple-element.190, f32[1,960,384]{2,0,1:T(1,128)S(1)} %copy.168, s32[]{:T(128)S(6)} %copy.176, s32[]{:T(128)} %constant.26.clone.1..sunk, s32[]{:T(128)} %constant.26.clone.1..sunk) | dynamic-update-slice | bytes 2949124 | tf_op jit(solution)/shard_map/while/body/jit(dynamic_update_index_in_dim)/dynamic_update_slice | solution.py:150
  306.5 13.6 %multiply_reduce_fusion.2 = (f32[4,960]{1,0:T(4,128)S(1)}, f32[4,960,2048]{2,1,0:T(8,128)}) fusion(bf16[960,4,96]{0,2,1:T(8,128)(2,1)} %bitcast.96, bf16[2048,4,96]{0,2,1:T(8,128)(2,1)S(1)} %bitcast.95), kind=kOutput, calls=%fused_computation.5.clone.1 | convolution fusion | flops 1525674240 | bytes 33782784 | tf_op jit(solution)/shard_map/while/body/eval_jaxpr/rhd,phd->hrp/dot_general | solution.py:82
  320.1 13.8 %fusion.74 = f32[4,960]{1,0:T(4,128)S(1)} fusion(f32[4,960,2048]{2,1,0:T(8,128)} %get-tuple-element.176, f32[4,960]{1,0:T(4,128)S(1)} %get-tuple-element.177), kind=kLoop, calls=%fused_computation.6.clone.1 | loop fusion | flops 23589120 | bytes 31488000 | tf_op jit(solution)/shard_map/while/body/eval_jaxpr/reduce_sum | solution.py:87
  333.9 12.8 %bitcast_divide_fusion.2 = f32[960,4,96]{0,2,1:T(8,128)S(1)} fusion(bf16[2048,4,96]{0,2,1:T(8,128)(2,1)S(1)} %bitcast.97, f32[4,960,2048]{2,1,0:T(8,128)} %get-tuple-element.176, f32[4,960]{1,0:T(4,128)S(1)} %get-tuple-element.177, f32[960,4]{0,1:T(4,128)S(1)} %bitcast.113), kind=kOutput, calls=%fused_computation.9.clone.1 | convolution fusion | flops 1533911040 | bytes 34535424 | tf_op jit(solution)/shard_map/while/body/eval_jaxpr/hrp,phd->rhd/dot_general | solution.py:89
  346.7 2.3 copy.168
  349.0 28.5 %dynamic_update_slice.16 = f32[2,960,384]{2,0,1:T(2,128)} dynamic-update-slice(f32[2,960,384]{2,0,1:T(2,128)} %get-tuple-element.190, f32[1,960,384]{2,0,1:T(1,128)S(1)} %copy.168, s32[]{:T(128)S(6)} %copy.176, s32[]{:T(128)} %constant.26.clone.1..sunk, s32[]{:T(128)} %constant.26.clone.1..sunk) | dynamic-update-slice | bytes 2949124 | tf_op jit(solution)/shard_map/while/body/jit(dynamic_update_index_in_dim)/dynamic_update_slice | solution.py:150
  380.6 3.3 all-to-all-start.1
  386.3 3.0 all-to-all-done.1
  389.3 7.8 %all_to_all.63 = f32[8,1,960]{2,1,0:T(1,128)S(1)} all-to-all(f32[8,1,960]{2,1,0:T(1,128)S(1)} %reshape.331), channel_id=1, replica_groups=mesh['tok'=8,'head'=16] {'tok'}, dimensions={0} | all-to-all | bytes 61440 | tf_op jit(solution)/shard_map/all_to_all | solution.py:153
  397.1 4.4 all-to-all-start.3
  403.7 2.7 copy-done.3
  416.6 21.3 %all-to-all-done.3 = f32[2,960,384]{2,0,1:T(2,128)} async-done(((f32[2,960,384]{2,0,1:T(2,128)}), f32[2,960,384]{2,0,1:T(2,128)}, u32[]{:S(2)}, u32[]{:S(2)}) %all-to-all-start.3) | async-done | bytes 2949152 | tf_op jit(solution)/shard_map/all_to_all | solution.py:152
  440.1 3.6 reshape.327
  443.7 3.9 gather_fusion.3
  448.6 5.3 divide_convert_fusion
  453.9 7.7 %fusion.56 = f32[640,6144]{1,0:T(8,128)} fusion(bf16[640,384]{0,1:T(8,128)(2,1)S(1)} %bitcast.114, bf16[384,6144]{1,0:T(8,128)(2,1)S(1)} %bitcast.107), kind=kOutput, calls=%fused_computation.98 | convolution fusion | flops 3019898880 | bytes 20938752 | tf_op jit(solution)/shard_map/dot_general | solution.py:168
  462.4 104.5 %reduce-scatter.2.cloned.1.call-done = f32[640,384]{1,0:T(8,128)} async-done(((f32[640,6144]{1,0:T(8,128)}), f32[640,384]{1,0:T(8,128)}) %reduce-scatter.2.cloned.1.call-update) | async-done | bytes 983056 | tf_op jit(solution)/shard_map/reduce_scatter | solution.py:169
  566.9 2.1 add_convert_fusion
  (117 shorter events, 50.7 us)
Async XLA Ops:
  6.5 81.3 %all-gather.3.cloned.1.call-start = ((), (), s32[]{:S(2)}) async-start(), calls=%async_computation.5 | async-start | bytes 8355840 | tf_op jit(solution)/shard_map/all_gather | solution.py:125
  7.3 155.5 %all-gather.5.cloned.1.call-start = ((), (), s32[]{:S(2)}) async-start(), calls=%async_computation.6 | async-start | bytes 15925248 | tf_op jit(solution)/shard_map/all_gather | solution.py:129
  13.2 0.7 copy-start.13
  14.1 171.3 %copy-start.8 = (f32[640,12]{0,1:T(8,128)}, f32[640,12]{0,1:T(8,128)S(1)}, u32[]{:S(2)}) copy-start(f32[640,12]{0,1:T(8,128)S(1)} %get-tuple-element.121) | copy-start | bytes 92164
  14.1 171.3 %copy-start.10 = (f32[640,12]{0,1:T(8,128)}, f32[640,12]{0,1:T(8,128)S(1)}, u32[]{:S(2)}) copy-start(f32[640,12]{0,1:T(8,128)S(1)} %get-tuple-element.122) | copy-start | bytes 92164
  87.8 5.5 copy-start.1
  87.8 75.0 %copy-start.17 = (f32[6144]{0:T(1024)S(1)}, f32[6144]{0:T(1024)}, u32[]{:S(2)}) copy-start(f32[6144]{0:T(1024)} %param.16) | copy-start | bytes 73732
  87.8 75.0 %copy-start.18 = (f32[6144]{0:T(1024)S(1)}, f32[6144]{0:T(1024)}, u32[]{:S(2)}) copy-start(f32[6144]{0:T(1024)} %param.15) | copy-start | bytes 73732
  183.9 1.9 copy-start.2
  185.9 6.7 %copy-start.6 = (bf16[640,4,96]{0,2,1:T(8,128)(2,1)}, bf16[640,4,96]{0,2,1:T(8,128)(2,1)S(1)}, u32[]{:S(2)}) copy-start(bf16[640,4,96]{0,2,1:T(8,128)(2,1)S(1)} %maximum_convert_fusion) | copy-start | bytes 1474564
  194.1 24.0 %all-to-all-start = ((bf16[16,120,384]{2,1,0:T(8,128)(2,1)}), bf16[16,120,384]{2,1,0:T(8,128)(2,1)S(1)}, u32[]{:S(2)}, u32[]{:S(2)}) async-start(bf16[16,120,384]{2,1,0:T(8,128)(2,1)} %broadcast_select_fusion), calls=%async_computation | async-start | bytes 2949120 | tf_op jit(solution)/shard_map/all_to_all | solution.py:149
  241.0 13.8 %copy-start = (bf16[1,2048,384]{1,2,0:T(8,128)(2,1)S(1)}, bf16[1,2048,384]{1,2,0:T(8,128)(2,1)}, u32[]{:S(2)}) copy-start(bf16[1,2048,384]{1,2,0:T(8,128)(2,1)} %copy.165) | copy-start | bytes 4718596 | tf_op jit(solution)/shard_map/while
  320.1 13.8 %copy-start = (bf16[1,2048,384]{1,2,0:T(8,128)(2,1)S(1)}, bf16[1,2048,384]{1,2,0:T(8,128)(2,1)}, u32[]{:S(2)}) copy-start(bf16[1,2048,384]{1,2,0:T(8,128)(2,1)} %copy.165) | copy-start | bytes 4718596 | tf_op jit(solution)/shard_map/while
  377.6 24.3 %copy-start.14 = (s32[640]{0:T(1024)S(1)}, s32[640]{0:T(1024)}, u32[]{:S(2)}) copy-start(s32[640]{0:T(1024)} %copy-done.13) | copy-start | bytes 7684
  377.6 24.3 %copy-start.15 = (s32[640]{0:T(1024)S(1)}, s32[640]{0:T(1024)}, u32[]{:S(2)}) copy-start(s32[640]{0:T(1024)} %get-tuple-element.128) | copy-start | bytes 7684
  377.6 24.3 %copy-start.12 = (s32[640]{0:T(1024)S(1)}, s32[640]{0:T(1024)}, u32[]{:S(2)}) copy-start(s32[640]{0:T(1024)} %get-tuple-element.89) | copy-start | bytes 7684
  377.6 24.6 %copy-start.4 = (f32[640,4,96]{0,2,1:T(8,128)S(1)}, f32[640,4,96]{0,2,1:T(8,128)}, u32[]{:S(2)}) copy-start(f32[640,4,96]{0,2,1:T(8,128)} %get-tuple-element.125) | copy-start | bytes 2949124
  377.6 24.7 %copy-start.9 = (f32[640,12]{0,1:T(8,128)S(1)}, f32[640,12]{0,1:T(8,128)}, u32[]{:S(2)}) copy-start(f32[640,12]{0,1:T(8,128)} %copy-done.8) | copy-start | bytes 92164
  377.6 24.7 %copy-start.11 = (f32[640,12]{0,1:T(8,128)S(1)}, f32[640,12]{0,1:T(8,128)}, u32[]{:S(2)}) copy-start(f32[640,12]{0,1:T(8,128)} %copy-done.10) | copy-start | bytes 92164
  377.6 24.7 %copy-start.7 = (bf16[640,4,96]{0,2,1:T(8,128)(2,1)S(1)}, bf16[640,4,96]{0,2,1:T(8,128)(2,1)}, u32[]{:S(2)}) copy-start(bf16[640,4,96]{0,2,1:T(8,128)(2,1)} %copy-done.6) | copy-start | bytes 1474564
  380.6 8.7 %all-to-all-start.1 = ((f32[8,1,960]{2,1,0:T(1,128)}), f32[8,1,960]{2,1,0:T(1,128)S(1)}, u32[]{:S(2)}, u32[]{:S(2)}) async-start(f32[8,1,960]{2,1,0:T(1,128)} %reshape.329), calls=%async_computation.1 | async-start | bytes 65536 | tf_op jit(solution)/shard_map/all_to_all | solution.py:154
  397.1 40.8 %all-to-all-start.3 = ((f32[2,960,384]{2,0,1:T(2,128)}), f32[2,960,384]{2,0,1:T(2,128)}, u32[]{:S(2)}, u32[]{:S(2)}) async-start(f32[2,960,384]{2,0,1:T(2,128)} %get-tuple-element.46), calls=%async_computation.3 | async-start | bytes 5898240 | tf_op jit(solution)/shard_map/all_to_all | solution.py:152
  401.6 165.3 %reduce-scatter.2.cloned.1.call-start = ((), (), s32[]{:S(2)}) async-start(), calls=%async_computation.7 | async-start | bytes 16711680 | tf_op jit(solution)/shard_map/reduce_scatter | solution.py:169
  403.7 2.7 copy-start.3
  447.6 6.3 %slice-start = ((s8[4718592]{0:T(1024)(128)(4,1)}), s8[524288]{0:T(1024)(128)(4,1)S(1)}, s32[]{:S(2)}) async-start(s8[4718592]{0:T(1024)(128)(4,1)} %bitcast.106), calls=%async_computation.8 | async-start | bytes 1048576
  448.6 5.3 slice-start.1
  461.7 0.7 copy-start.16
  461.7 105.2 %copy-start.5 = (bf16[640,384]{1,0:T(8,128)(2,1)S(1)}, bf16[640,384]{1,0:T(8,128)(2,1)}, u32[]{:S(2)}) copy-start(bf16[640,384]{1,0:T(8,128)(2,1)} %param.14) | copy-start | bytes 1474564
Sparse Core Ops, SparseCore 0:
  9.5 78.2 all-gather.2
  89.5 73.2 all-gather.4
  461.8 105.0 reduce-scatter.1
where the time goes:
time: 581 us; the launch traced here: 576 us
  waiting for transfers between devices  291 us (50%)
  local copies, waits for them, and re-layouts  118 us (20%)
  matrix products  85.3 us (15%)
  other arithmetic  47.4 us (8%)
  between operations  13.6 us (2%)
  starting transfers between devices  11.8 us (2%)
  blocking collectives  7.8 us (1%)
    reduce_scatter x1, waiting for transfers between devices, on_device(): lax.psum_scatter(partial_out, 'head', scatter_dimension=1, tiled=True)  105 us
    all_gather x1, waiting for transfers between devices, on_device(): full_rows = lax.all_gather(hidden_states, 'head', axis=1, tiled=True)  73.6 us
    all_gather x1, waiting for transfers between devices, on_device(): lax.all_gather(qkv_weight, 'tok', axis=0, tiled=True)  67.3 us
    dynamic_update_slice x6, local copies, waits for them, and re-layouts, on_device(): lax.map(prefix_slot, (incoming, prefix_keys, prefix_values))  61.7 us
    reduce_sum x2, other arithmetic, prefix_slot(): row_mass = jnp.sum(weights, axis=-1)  27.7 us
    dot_general x2, matrix products, prefix_slot(): jnp.einsum('rhd,phd->hrp', query_heads, key_heads, preferred_element_type...  27.2 us
    dot_general x2, matrix products, prefix_slot(): jnp.einsum('hrp,phd->rhd', weights.astype(jnp.bfloat16), value_heads, pre...  25.5 us
    all_to_all x1, waiting for transfers between devices, on_device(): lax.all_to_all(pre_all, 'tok', split_axis=1, concat_axis=0, tiled=True)  21.3 us
  transfers between devices with their start and end apart: 6, of which 6 were waited for; matrix products, arithmetic and copies ran while one was open for 5% of the time, Pallas kernels for 0%

commit v1 on v0

--- a/solution.py
+++ b/solution.py
@@ -2,6 +2,8 @@
 import jax.numpy as jnp
 from jax import lax
 from jax.sharding import PartitionSpec as P
+from jax.experimental import pallas as pl
+from jax.experimental.pallas import tpu as pltpu
 
 HS = 96
 
@@ -99,6 +101,59 @@
         jnp.transpose(row_peak),
         jnp.transpose(row_mass),
     )
+
+
+def prefix_kernel(q_ref, k_ref, v_ref, o_ref, peak_ref, mass_ref):
+    local_heads = q_ref.shape[-1] // HS
+    peaks = []
+    masses = []
+    for head in range(local_heads):
+        cols = pl.ds(head * HS, HS)
+        scores = lax.dot_general(
+            q_ref[:, cols],
+            k_ref[:, cols],
+            (((1,), (1,)), ((), ())),
+            preferred_element_type=jnp.float32,
+        ) * HS ** (-0.5)
+        row_peak = jnp.max(scores, axis=-1, keepdims=True)
+        weights = jnp.exp(scores - row_peak)
+        row_mass = jnp.sum(weights, axis=-1, keepdims=True)
+        blended = jnp.dot(
+            weights.astype(jnp.bfloat16), v_ref[:, cols], preferred_element_type=jnp.float32
+        )
+        o_ref[:, cols] = blended / row_mass
+        peaks.append(row_peak)
+        masses.append(row_mass)
+    peak_ref[...] = jnp.concatenate(peaks, axis=-1)
+    mass_ref[...] = jnp.concatenate(masses, axis=-1)
+
+
+def prefix_attention(queries_in, keys_in, values_in):
+    slot_count, row_total, local_width = queries_in.shape
+    prefix_length = keys_in.shape[1]
+    local_heads = local_width // HS
+    row_tile = row_total // 2 if row_total % 16 == 0 else row_total
+    grid = (slot_count, row_total // row_tile)
+    return pl.pallas_call(
+        prefix_kernel,
+        grid=grid,
+        in_specs=[
+            pl.BlockSpec((None, row_tile, local_width), lambda s, r: (s, r, 0)),
+            pl.BlockSpec((None, prefix_length, local_width), lambda s, r: (s, 0, 0)),
+            pl.BlockSpec((None, prefix_length, local_width), lambda s, r: (s, 0, 0)),
+        ],
+        out_specs=[
+            pl.BlockSpec((None, row_tile, local_width), lambda s, r: (s, r, 0)),
+            pl.BlockSpec((None, row_tile, local_heads), lambda s, r: (s, r, 0)),
+            pl.BlockSpec((None, row_tile, local_heads), lambda s, r: (s, r, 0)),
+        ],
+        out_shape=[
+            jax.ShapeDtypeStruct((slot_count, row_total, local_width), jnp.float32),
+            jax.ShapeDtypeStruct((slot_count, row_total, local_heads), jnp.float32),
+            jax.ShapeDtypeStruct((slot_count, row_total, local_heads), jnp.float32),
+        ],
+        compiler_params=pltpu.CompilerParams(vmem_limit_bytes=60 * 1024 * 1024),
+    )(queries_in, keys_in, values_in)
 
 
 def on_device(
@@ -147,7 +202,7 @@
     flat_query = queries.reshape(tok_rows, local_width)
     outgoing = jnp.where(live_slot[..., None], flat_query[source_rows], jnp.zeros((), jnp.bfloat16))
     incoming = lax.all_to_all(outgoing, "tok", split_axis=0, concat_axis=1, tiled=True)
-    pre_all, peak_all, mass_all = lax.map(prefix_slot, (incoming, prefix_keys, prefix_values))
+    pre_all, peak_all, mass_all = prefix_attention(incoming, prefix_keys, prefix_values)
     returned = (
         lax.all_to_all(pre_all, "tok", split_axis=1, concat_axis=0, tiled=True),
         lax.all_to_all(peak_all, "tok", split_axis=1, concat_axis=0, tiled=True),

time: 581 us -> 469 us (0.81)
  local copies, waits for them, and re-layouts: 118 us -> 59.8 us
  matrix products: 85.3 us -> 32.5 us
  other arithmetic: 47.4 us -> 17.3 us
  Pallas kernels: 0 us -> 29.7 us
  waiting for transfers between devices: 291 us -> 271 us
  blocking collectives: 7.8 us -> 24.4 us
    dynamic_update_slice x6 -> x0, local copies, waits for them, and re-layouts: 61.7 us -> none  [on_device(): lax.map(prefix_slot, (incoming, prefix_keys, prefix_values))]
    dot_general x4 -> x0, matrix products: 52.8 us -> none  [the longest x2 27.2 us: prefix_slot(): jnp.einsum('rhd,phd->hrp', query_heads, key_heads, preferred_element_type...]
    pallas_call x0 -> x1, Pallas kernels: none -> 29.7 us  [prefix_attention(): pl.pallas_call(prefix_kernel, grid=grid, in_specs=[pl.BlockSpec((None, ro...]
    reduce_sum x2 -> x0, other arithmetic: 27.7 us -> none  [prefix_slot(): row_mass = jnp.sum(weights, axis=-1)]
    all_to_all x1, waiting for transfers between devices: 20.2 us -> 1.35 us  [on_device(): lax.all_to_all(peak_all, 'tok', split_axis=1, concat_axis=0, tiled=True)]
    all_to_all x1, blocking collectives: 7.8 us -> 24.4 us  [on_device(): lax.all_to_all(outgoing, 'tok', split_axis=0, concat_axis=1, tiled=True)]
    dynamic_slice x12 -> x0, local copies, waits for them, and re-layouts: 15.9 us -> none  [on_device(): lax.map(prefix_slot, (incoming, prefix_keys, prefix_values))]
    pallas_call x0 -> x3, local copies, waits for them, and re-layouts: none -> 9.67 us  [prefix_attention(): pl.pallas_call(prefix_kernel, grid=grid, in_specs=[pl.BlockSpec((None, ro...]
  transfers between devices with their start and end apart: 6 -> 6, of which waited for: 6 -> 5; matrix products, arithmetic and copies ran while one was open for 5% -> 7% of each run, Pallas kernels for 0% -> 0%
where the time goes in v1:
time: 469 us; the launch traced here: 460 us
  waiting for transfers between devices  271 us (58%)
  local copies, waits for them, and re-layouts  59.8 us (13%)
  matrix products  32.5 us (7%)
  Pallas kernels  29.7 us (6%)
  blocking collectives  24.4 us (5%)
  other arithmetic  17.3 us (4%)
  between operations  13.7 us (3%)
  starting transfers between devices  11.8 us (3%)
    reduce_scatter x1, waiting for transfers between devices, on_device(): lax.psum_scatter(partial_out, 'head', scatter_dimension=1, tiled=True)  105 us
    all_gather x1, waiting for transfers between devices, on_device(): full_rows = lax.all_gather(hidden_states, 'head', axis=1, tiled=True)  74.8 us
    all_gather x1, waiting for transfers between devices, on_device(): lax.all_gather(qkv_weight, 'tok', axis=0, tiled=True)  67.3 us
    pallas_call x1, Pallas kernels, prefix_attention(): pl.pallas_call(prefix_kernel, grid=grid, in_specs=[pl.BlockSpec((None, ro...  29.7 us
    all_to_all x1, blocking collectives, on_device(): lax.all_to_all(outgoing, 'tok', split_axis=0, concat_axis=1, tiled=True)  24.4 us
    all_to_all x1, waiting for transfers between devices, on_device(): lax.all_to_all(pre_all, 'tok', split_axis=1, concat_axis=0, tiled=True)  21.5 us
    dot_general x1, matrix products, on_device(): jnp.dot(normed, lax.all_gather(qkv_weight, 'tok', axis=0, tiled=True), pr...  18.1 us
    unnamed x28, local copies, waits for them, and re-layouts  11.7 us
  transfers between devices with their start and end apart: 6, of which 5 were waited for; matrix products, arithmetic and copies ran while one was open for 7% of the time, Pallas kernels for 0%

profile of v1, /device:TPU:0, one launch (start us, length us, event | category | flops | bytes accessed | tf_op | source)
XLA Modules:
  0.0 460.3 jit_solution(5029057122505487221)
XLA Ops:
  13.0 74.8 %all-gather.3.cloned.1.call-done = bf16[640,6144]{1,0:T(8,128)(2,1)} async-done(((bf16[640,384]{1,0:T(8,128)(2,1)}), bf16[640,6144]{1,0:T(8,128)(2,1)}) %all-gather.3.cloned.1.call-update) | async-done | bytes 7864336 | tf_op jit(solution)/shard_map/all_gather | solution.py:180
  87.8 4.5 convert_reduce_fusion
  93.3 2.2 fusion.2
  95.4 67.3 %all-gather.5.cloned.1.call-done = bf16[6144,1152]{1,0:T(8,128)(2,1)} async-done(((bf16[768,1152]{1,0:T(8,128)(2,1)}), bf16[6144,1152]{1,0:T(8,128)(2,1)}) %all-gather.5.cloned.1.call-update) | async-done | bytes 14155792 | tf_op jit(solution)/shard_map/all_gather | solution.py:184
  162.7 18.1 %fusion.15 = f32[640,1152]{1,0:T(8,128)} fusion(bf16[6144,1152]{1,0:T(8,128)(2,1)} %all-gather.5.cloned.1.call-done, bf16[640,6144]{1,0:T(8,128)(2,1)} %all-gather.3.cloned.1.call-done, f32[6144]{0:T(1024)S(1)} %copy-done.8, f32[6144]{0:T(1024)S(1)} %copy-done.9, f32[640]{0:T(1024)S(1)} %add_rsqrt_fusion, f32[640]{0:T(1024)S(1)} %broadcast_multiply_fusion.1, ...), kind=kOutput, calls=%fused_computation.22 | convolution fusion | flops 9084026880 | bytes 25028096 | tf_op jit(solution)/shard_map/dot_general | solution.py:182
  180.8 3.1 copy.84
  186.1 6.4 %gather_fusion = bf16[1920,384]{1,0:T(8,128)(2,1)S(1)} fusion(bf16[640,384]{1,0:T(8,128)(2,1)S(1)} %copy.86, s32[2048]{0:T(1024)S(1)} %pad_clamp_fusion), kind=kCustom, calls=%fused_computation | custom fusion | bytes 2956800 | tf_op jit(solution)/shard_map/gather | solution.py:203
  192.9 24.4 %all_to_all.63 = bf16[16,120,384]{2,1,0:T(8,128)(2,1)S(1)} all-to-all(bf16[16,120,384]{2,1,0:T(8,128)(2,1)S(1)} %broadcast_select_fusion), channel_id=1, replica_groups=mesh['tok'=8,'head'=16] {'tok'}, dimensions={0} | all-to-all | bytes 2949120 | tf_op jit(solution)/shard_map/all_to_all | solution.py:204
  218.6 29.7 %shard_map.118 = (f32[2,960,384]{2,1,0:T(8,128)}, f32[2,960,4]{2,1,0:T(8,128)}, f32[2,960,4]{2,1,0:T(8,128)}) custom-call(bf16[2,960,384]{2,1,0:T(8,128)(2,1)} %bitcast.68, bf16[2,2048,384]{2,1,0:T(8,128)(2,1)} %k_ref.1, bf16[2,2048,384]{2,1,0:T(8,128)(2,1)} %v_ref.1), custom_call_target="tpu_custom_call" | custom-call | tf_op jit(solution)/shard_map/pallas_call | solution.py:137
  248.4 2.0 copy.114
  250.3 2.0 reshape.314
  252.4 3.3 all-to-all-start.2
  255.7 2.0 copy.115
  257.7 2.0 reshape.312
  261.1 3.6 all-to-all-start.1
  264.7 5.7 %copy.96 = f32[2,960,384]{2,0,1:T(2,128)} copy(f32[2,960,384]{2,1,0:T(8,128)} %get-tuple-element.10) | data formatting | bytes 5898240 | tf_op jit(solution)/shard_map/pallas_call | solution.py:137
  270.4 4.8 %all-to-all-start.3 = ((f32[2,960,384]{2,0,1:T(2,128)}), f32[2,960,384]{2,0,1:T(2,128)}, u32[]{:S(2)}, u32[]{:S(2)}) async-start(f32[2,960,384]{2,0,1:T(2,128)} %copy.96), calls=%async_computation.3 | async-start | bytes 5898240 | tf_op jit(solution)/shard_map/all_to_all | solution.py:207
  277.1 2.7 copy-done.2
  279.8 1.4 fusion.14
  282.6 1.4 reshape.315
  284.1 1.9 gather_fusion.2
  286.8 1.4 reshape.313
  288.3 1.7 gather_fusion.1
  290.2 21.5 %all-to-all-done.3 = f32[2,960,384]{2,0,1:T(2,128)} async-done(((f32[2,960,384]{2,0,1:T(2,128)}), f32[2,960,384]{2,0,1:T(2,128)}, u32[]{:S(2)}, u32[]{:S(2)}) %all-to-all-start.3) | async-done | bytes 2949152 | tf_op jit(solution)/shard_map/all_to_all | solution.py:207
  311.7 5.4 %copy.97 = f32[2,8,120,384]{2,0,1,3:T(2,128)S(1)} copy(f32[2,8,120,384]{3,0,2,1:T(2,128)} %bitcast.19) | data formatting | bytes 5898240 | tf_op jit(solution)/shard_map/all_to_all | solution.py:207
  317.1 6.2 %reshape.277 = f32[1920,4,96]{0,2,1:T(8,128)} reshape(f32[8,2,120,384]{2,1,0,3:T(2,128)S(1)} %bitcast.63) | data formatting | bytes 5898240 | tf_op jit(solution)/shard_map/reshape | solution.py:213
  323.3 4.9 %copy.98 = f32[1920,4,96]{2,1,0:T(4,128)} copy(f32[1920,4,96]{0,2,1:T(8,128)} %reshape.277) | data formatting | bytes 5898240 | tf_op jit(solution)/shard_map/reshape | solution.py:213
  328.2 3.9 gather_fusion.3
  333.1 5.3 %divide_convert_fusion = bf16[640,4,96]{0,2,1:T(8,128)(2,1)S(1)} fusion(f32[640,4,96]{0,2,1:T(8,128)S(1)} %copy.99, f32[4,640,640]{1,2,0:T(8,128)} %copy-done.2, f32[4,640]{1,0:T(4,128)S(1)} %get-tuple-element.27, pred[640,640]{0,1:T(8,128)(4,1)S(1)} %copy-done.6, f32[640,4]{0,1:T(4,128)S(1)} %get-tuple-element.16, f32[640,4]{0,1:T(4,128)S(1)} %bitcast.77, ...), kind=kOutput, calls=%fused_computation.34 | convolution fusion | flops 322600960 | bytes 8980480 | tf_op jit(solution)/shard_map/hij,jhd->ihd/dot_general | solution.py:64
  338.4 7.7 %fusion.49 = f32[640,6144]{1,0:T(8,128)} fusion(bf16[640,384]{0,1:T(8,128)(2,1)S(1)} %bitcast.76, bf16[384,6144]{1,0:T(8,128)(2,1)S(1)} %bitcast.70), kind=kOutput, calls=%fused_computation.88 | convolution fusion | flops 3019898880 | bytes 20938752 | tf_op jit(solution)/shard_map/dot_general | solution.py:223
  346.8 104.6 %reduce-scatter.2.cloned.1.call-done = f32[640,384]{1,0:T(8,128)} async-done(((f32[640,6144]{1,0:T(8,128)}), f32[640,384]{1,0:T(8,128)}) %reduce-scatter.2.cloned.1.call-update) | async-done | bytes 983056 | tf_op jit(solution)/shard_map/reduce_scatter | solution.py:224
  451.4 2.1 add_convert_fusion
  (71 shorter events, 18.4 us)
Async XLA Ops:
  6.5 81.3 %all-gather.3.cloned.1.call-start = ((), (), s32[]{:S(2)}) async-start(), calls=%async_computation.5 | async-start | bytes 8355840 | tf_op jit(solution)/shard_map/all_gather | solution.py:180
  7.3 155.5 %all-gather.5.cloned.1.call-start = ((), (), s32[]{:S(2)}) async-start(), calls=%async_computation.6 | async-start | bytes 15925248 | tf_op jit(solution)/shard_map/all_gather | solution.py:184
  87.8 5.5 %copy-start = (bf16[640,6144]{1,0:T(8,128)(2,1)S(1)}, bf16[640,6144]{1,0:T(8,128)(2,1)}, u32[]{:S(2)}) copy-start(bf16[640,6144]{1,0:T(8,128)(2,1)} %all-gather.3.cloned.1.call-done) | copy-start | bytes 23592964
  87.8 75.0 %copy-start.8 = (f32[6144]{0:T(1024)S(1)}, f32[6144]{0:T(1024)}, u32[]{:S(2)}) copy-start(f32[6144]{0:T(1024)} %param.14) | copy-start | bytes 73732
  87.8 75.0 %copy-start.9 = (f32[6144]{0:T(1024)S(1)}, f32[6144]{0:T(1024)}, u32[]{:S(2)}) copy-start(f32[6144]{0:T(1024)} %param.13) | copy-start | bytes 73732
  183.9 1.9 copy-start.1
  252.4 8.7 %all-to-all-start.2 = ((f32[8,1,960]{2,1,0:T(1,128)}), f32[8,1,960]{2,1,0:T(1,128)S(1)}, u32[]{:S(2)}, u32[]{:S(2)}) async-start(f32[8,1,960]{2,1,0:T(1,128)} %reshape.314), calls=%async_computation.2 | async-start | bytes 65536 | tf_op jit(solution)/shard_map/all_to_all | solution.py:208
  257.7 17.9 %copy-start.3 = (f32[640,4,96]{0,2,1:T(8,128)S(1)}, f32[640,4,96]{0,2,1:T(8,128)}, u32[]{:S(2)}) copy-start(f32[640,4,96]{0,2,1:T(8,128)} %get-tuple-element.29) | copy-start | bytes 2949124
  261.1 9.3 %all-to-all-start.1 = ((f32[8,1,960]{2,1,0:T(1,128)}), f32[8,1,960]{2,1,0:T(1,128)S(1)}, u32[]{:S(2)}, u32[]{:S(2)}) async-start(f32[8,1,960]{2,1,0:T(1,128)} %reshape.312), calls=%async_computation.1 | async-start | bytes 65536 | tf_op jit(solution)/shard_map/all_to_all | solution.py:209
  270.4 41.2 %all-to-all-start.3 = ((f32[2,960,384]{2,0,1:T(2,128)}), f32[2,960,384]{2,0,1:T(2,128)}, u32[]{:S(2)}, u32[]{:S(2)}) async-start(f32[2,960,384]{2,0,1:T(2,128)} %copy.96), calls=%async_computation.3 | async-start | bytes 5898240 | tf_op jit(solution)/shard_map/all_to_all | solution.py:207
  275.2 176.2 %reduce-scatter.2.cloned.1.call-start = ((), (), s32[]{:S(2)}) async-start(), calls=%async_computation.7 | async-start | bytes 16711680 | tf_op jit(solution)/shard_map/reduce_scatter | solution.py:224
  275.6 5.7 %copy-start.5 = (pred[640,640]{0,1:T(8,128)(4,1)}, pred[640,640]{0,1:T(8,128)(4,1)S(1)}, u32[]{:S(2)}) copy-start(pred[640,640]{0,1:T(8,128)(4,1)S(1)} %fusion.21) | copy-start | bytes 1228804
  277.1 2.7 copy-start.2
  323.3 9.8 %copy-start.6 = (pred[640,640]{0,1:T(8,128)(4,1)S(1)}, pred[640,640]{0,1:T(8,128)(4,1)}, u32[]{:S(2)}) copy-start(pred[640,640]{0,1:T(8,128)(4,1)} %copy-done.5) | copy-start | bytes 1228804
  328.2 10.2 %slice-start = ((s8[4718592]{0:T(1024)(128)(4,1)}), s8[524288]{0:T(1024)(128)(4,1)S(1)}, s32[]{:S(2)}) async-start(s8[4718592]{0:T(1024)(128)(4,1)} %bitcast.69), calls=%async_computation.8 | async-start | bytes 1048576
  333.1 5.3 %slice-start.1 = ((s8[4718592]{0:T(1024)(128)(4,1)}), s8[4194304]{0:T(1024)(128)(4,1)S(1)}, s32[]{:S(2)}) async-start(s8[4718592]{0:T(1024)(128)(4,1)} %bitcast.69), calls=%async_computation.9 | async-start | bytes 8388608
  346.2 0.7 copy-start.7
  346.2 105.2 %copy-start.4 = (bf16[640,384]{1,0:T(8,128)(2,1)S(1)}, bf16[640,384]{1,0:T(8,128)(2,1)}, u32[]{:S(2)}) copy-start(bf16[640,384]{1,0:T(8,128)(2,1)} %param.12) | copy-start | bytes 1474564
Sparse Core Ops, SparseCore 0:
  9.5 78.2 all-gather.2
  89.5 73.2 all-gather.4
  346.3 105.0 reduce-scatter.1

commit v2 on v1

--- a/solution.py
+++ b/solution.py
@@ -221,7 +221,9 @@
     )[..., None]
     attention = combined.reshape(tok_rows, local_width).astype(jnp.bfloat16)
     partial_out = jnp.dot(attention, dense_weight, preferred_element_type=jnp.float32)
-    summed = lax.psum_scatter(partial_out, "head", scatter_dimension=1, tiled=True)
+    summed = lax.psum_scatter(
+        partial_out.astype(jnp.bfloat16), "head", scatter_dimension=1, tiled=True
+    ).astype(jnp.float32)
     return (hidden_states.astype(jnp.float32) + dense_bias.astype(jnp.float32) + summed).astype(
         jnp.bfloat16
     )

time: 469 us -> 457 us (0.974)
  waiting for transfers between devices: 271 us -> 249 us
  local copies, waits for them, and re-layouts: 59.8 us -> 71.6 us
    reduce_scatter x1 -> x0, waiting for transfers between devices: 105 us -> none  [on_device(): lax.psum_scatter(partial_out, 'head', scatter_dimension=1, tiled=True)]
    unnamed x3 -> x4, waiting for transfers between devices: 1.42 us -> 84.5 us
    unnamed x28 -> x30, local copies, waits for them, and re-layouts: 11.7 us -> 23.4 us
where the time goes in v2:
time: 457 us; the launch traced here: 448 us
  waiting for transfers between devices  249 us (54%)
  local copies, waits for them, and re-layouts  71.6 us (16%)
  matrix products  31.1 us (7%)
  Pallas kernels  29.7 us (6%)
  blocking collectives  24.4 us (5%)
  other arithmetic  16.2 us (4%)
  between operations  13.7 us (3%)
  starting transfers between devices  11.8 us (3%)
    unnamed x4, waiting for transfers between devices  84.5 us
    all_gather x1, waiting for transfers between devices, on_device(): full_rows = lax.all_gather(hidden_states, 'head', axis=1, tiled=True)  74.8 us
    all_gather x1, waiting for transfers between devices, on_device(): lax.all_gather(qkv_weight, 'tok', axis=0, tiled=True)  67.3 us
    pallas_call x1, Pallas kernels, prefix_attention(): pl.pallas_call(prefix_kernel, grid=grid, in_specs=[pl.BlockSpec((None, ro...  29.7 us
    all_to_all x1, blocking collectives, on_device(): lax.all_to_all(outgoing, 'tok', split_axis=0, concat_axis=1, tiled=True)  24.4 us
    unnamed x30, local copies, waits for them, and re-layouts  23.4 us
    all_to_all x1, waiting for transfers between devices, on_device(): lax.all_to_all(pre_all, 'tok', split_axis=1, concat_axis=0, tiled=True)  21.5 us
    dot_general x1, matrix products, on_device(): jnp.dot(normed, lax.all_gather(qkv_weight, 'tok', axis=0, tiled=True), pr...  18.1 us
  transfers between devices with their start and end apart: 6, of which 5 were waited for; matrix products, arithmetic and copies ran while one was open for 7% of the time, Pallas kernels for 0%

profile of v2, /device:TPU:0, one launch (start us, length us, event | category | flops | bytes accessed | tf_op | source)
XLA Modules:
  0.0 448.1 jit_solution(12477362790782068494)
XLA Ops:
  13.0 74.8 %all-gather.3.cloned.1.call-done = bf16[640,6144]{1,0:T(8,128)(2,1)} async-done(((bf16[640,384]{1,0:T(8,128)(2,1)}), bf16[640,6144]{1,0:T(8,128)(2,1)}) %all-gather.3.cloned.1.call-update) | async-done | bytes 7864336 | tf_op jit(solution)/shard_map/all_gather | solution.py:180
  87.8 4.5 %convert_reduce_fusion = f32[640]{0:T(1024)S(1)} fusion(bf16[640,6144]{1,0:T(8,128)(2,1)} %all-gather.3.cloned.1.call-done), kind=kLoop, calls=%fused_computation.5 | loop fusion | flops 7863680 | bytes 7866880 | tf_op jit(solution)/shard_map/reduce_sum | solution.py:13
  93.3 2.2 fusion.2
  95.4 67.3 %all-gather.5.cloned.1.call-done = bf16[6144,1152]{1,0:T(8,128)(2,1)} async-done(((bf16[768,1152]{1,0:T(8,128)(2,1)}), bf16[6144,1152]{1,0:T(8,128)(2,1)}) %all-gather.5.cloned.1.call-update) | async-done | bytes 14155792 | tf_op jit(solution)/shard_map/all_gather | solution.py:184
  162.7 18.1 %fusion.15 = f32[640,1152]{1,0:T(8,128)} fusion(bf16[6144,1152]{1,0:T(8,128)(2,1)} %all-gather.5.cloned.1.call-done, bf16[640,6144]{1,0:T(8,128)(2,1)} %all-gather.3.cloned.1.call-done, f32[6144]{0:T(1024)S(1)} %copy-done.8, f32[6144]{0:T(1024)S(1)} %copy-done.9, f32[640]{0:T(1024)S(1)} %add_rsqrt_fusion, f32[640]{0:T(1024)S(1)} %broadcast_multiply_fusion.1, ...), kind=kOutput, calls=%fused_computation.23 | convolution fusion | flops 9084026880 | bytes 25028096 | tf_op jit(solution)/shard_map/dot_general | solution.py:182
  180.8 3.1 copy.84
  186.1 6.4 %gather_fusion = bf16[1920,384]{1,0:T(8,128)(2,1)S(1)} fusion(bf16[640,384]{1,0:T(8,128)(2,1)S(1)} %copy.86, s32[2048]{0:T(1024)S(1)} %pad_clamp_fusion), kind=kCustom, calls=%fused_computation | custom fusion | bytes 2956800 | tf_op jit(solution)/shard_map/gather | solution.py:203
  192.9 24.4 %all_to_all.63 = bf16[16,120,384]{2,1,0:T(8,128)(2,1)S(1)} all-to-all(bf16[16,120,384]{2,1,0:T(8,128)(2,1)S(1)} %broadcast_select_fusion), channel_id=1, replica_groups=mesh['tok'=8,'head'=16] {'tok'}, dimensions={0} | all-to-all | bytes 2949120 | tf_op jit(solution)/shard_map/all_to_all | solution.py:204
  218.6 29.7 %shard_map.118 = (f32[2,960,384]{2,1,0:T(8,128)}, f32[2,960,4]{2,1,0:T(8,128)}, f32[2,960,4]{2,1,0:T(8,128)}) custom-call(bf16[2,960,384]{2,1,0:T(8,128)(2,1)} %bitcast.71, bf16[2,2048,384]{2,1,0:T(8,128)(2,1)} %k_ref.1, bf16[2,2048,384]{2,1,0:T(8,128)(2,1)} %v_ref.1), custom_call_target="tpu_custom_call" | custom-call | tf_op jit(solution)/shard_map/pallas_call | solution.py:137
  248.4 2.0 copy.116
  250.3 2.0 reshape.316
  252.4 3.3 all-to-all-start.2
  255.7 2.0 copy.117
  257.7 2.0 reshape.314
  261.1 3.6 all-to-all-start.1
  264.7 5.7 %copy.96 = f32[2,960,384]{2,0,1:T(2,128)} copy(f32[2,960,384]{2,1,0:T(8,128)} %get-tuple-element.10) | data formatting | bytes 5898240 | tf_op jit(solution)/shard_map/pallas_call | solution.py:137
  270.4 4.8 %all-to-all-start.3 = ((f32[2,960,384]{2,0,1:T(2,128)}), f32[2,960,384]{2,0,1:T(2,128)}, u32[]{:S(2)}, u32[]{:S(2)}) async-start(f32[2,960,384]{2,0,1:T(2,128)} %copy.96), calls=%async_computation.3 | async-start | bytes 5898240 | tf_op jit(solution)/shard_map/all_to_all | solution.py:207
  277.1 2.7 copy-done.2
  279.8 1.4 fusion.14
  282.6 1.4 reshape.317
  284.1 1.9 gather_fusion.2
  286.8 1.4 reshape.315
  288.3 1.7 gather_fusion.1
  290.2 21.5 %all-to-all-done.3 = f32[2,960,384]{2,0,1:T(2,128)} async-done(((f32[2,960,384]{2,0,1:T(2,128)}), f32[2,960,384]{2,0,1:T(2,128)}, u32[]{:S(2)}, u32[]{:S(2)}) %all-to-all-start.3) | async-done | bytes 2949152 | tf_op jit(solution)/shard_map/all_to_all | solution.py:207
  311.7 5.4 %copy.97 = f32[2,8,120,384]{2,0,1,3:T(2,128)S(1)} copy(f32[2,8,120,384]{3,0,2,1:T(2,128)} %bitcast.19) | data formatting | bytes 5898240 | tf_op jit(solution)/shard_map/all_to_all | solution.py:207
  317.1 6.2 %reshape.277 = f32[1920,4,96]{0,2,1:T(8,128)} reshape(f32[8,2,120,384]{2,1,0,3:T(2,128)S(1)} %bitcast.66) | data formatting | bytes 5898240 | tf_op jit(solution)/shard_map/reshape | solution.py:213
  323.3 4.9 %copy.98 = f32[1920,4,96]{2,1,0:T(4,128)} copy(f32[1920,4,96]{0,2,1:T(8,128)} %reshape.277) | data formatting | bytes 5898240 | tf_op jit(solution)/shard_map/reshape | solution.py:213
  328.2 3.9 gather_fusion.3
  333.1 5.3 %divide_convert_fusion = bf16[640,4,96]{0,2,1:T(8,128)(2,1)S(1)} fusion(f32[640,4,96]{0,2,1:T(8,128)S(1)} %copy.99, f32[4,640,640]{1,2,0:T(8,128)} %copy-done.2, f32[4,640]{1,0:T(4,128)S(1)} %get-tuple-element.27, pred[640,640]{0,1:T(8,128)(4,1)S(1)} %copy-done.6, f32[640,4]{0,1:T(4,128)S(1)} %get-tuple-element.16, f32[640,4]{0,1:T(4,128)S(1)} %bitcast.81, ...), kind=kOutput, calls=%fused_computation.35 | convolution fusion | flops 322600960 | bytes 8980480 | tf_op jit(solution)/shard_map/hij,jhd->ihd/dot_general | solution.py:64
  338.4 6.4 %convolution_convert_fusion = bf16[640,6144]{1,0:T(8,128)(2,1)} fusion(bf16[640,384]{0,1:T(8,128)(2,1)S(1)} %bitcast.79, bf16[384,6144]{1,0:T(8,128)(2,1)S(1)} %bitcast.73), kind=kOutput, calls=%fused_computation.12 | convolution fusion | flops 3023831040 | bytes 13074432 | tf_op jit(solution)/shard_map/dot_general | solution.py:223
  344.8 10.5 %copy.103 = bf16[640,6144]{0,1:T(8,128)(2,1)} copy(bf16[640,6144]{1,0:T(8,128)(2,1)} %convolution_convert_fusion) | data formatting | bytes 15728640
  356.0 83.0 %reduce-scatter.4.cloned.1.call-done = bf16[384,640]{1,0:T(8,128)(2,1)} async-done(((bf16[6144,640]{1,0:T(8,128)(2,1)}), bf16[384,640]{1,0:T(8,128)(2,1)}) %reduce-scatter.4.cloned.1.call-update) | async-done | bytes 491536
  (73 shorter events, 20.6 us)
Async XLA Ops:
  6.5 81.3 %all-gather.3.cloned.1.call-start = ((), (), s32[]{:S(2)}) async-start(), calls=%async_computation.5 | async-start | bytes 8355840 | tf_op jit(solution)/shard_map/all_gather | solution.py:180
  7.3 155.5 %all-gather.5.cloned.1.call-start = ((), (), s32[]{:S(2)}) async-start(), calls=%async_computation.6 | async-start | bytes 15925248 | tf_op jit(solution)/shard_map/all_gather | solution.py:184
  87.8 5.5 %copy-start = (bf16[640,6144]{1,0:T(8,128)(2,1)S(1)}, bf16[640,6144]{1,0:T(8,128)(2,1)}, u32[]{:S(2)}) copy-start(bf16[640,6144]{1,0:T(8,128)(2,1)} %all-gather.3.cloned.1.call-done) | copy-start | bytes 23592964
  87.8 75.0 %copy-start.8 = (f32[6144]{0:T(1024)S(1)}, f32[6144]{0:T(1024)}, u32[]{:S(2)}) copy-start(f32[6144]{0:T(1024)} %param.14) | copy-start | bytes 73732
  87.8 75.0 %copy-start.9 = (f32[6144]{0:T(1024)S(1)}, f32[6144]{0:T(1024)}, u32[]{:S(2)}) copy-start(f32[6144]{0:T(1024)} %param.13) | copy-start | bytes 73732
  183.9 1.9 copy-start.1
  252.4 8.7 %all-to-all-start.2 = ((f32[8,1,960]{2,1,0:T(1,128)}), f32[8,1,960]{2,1,0:T(1,128)S(1)}, u32[]{:S(2)}, u32[]{:S(2)}) async-start(f32[8,1,960]{2,1,0:T(1,128)} %reshape.316), calls=%async_computation.2 | async-start | bytes 65536 | tf_op jit(solution)/shard_map/all_to_all | solution.py:208
  257.7 17.9 %copy-start.3 = (f32[640,4,96]{0,2,1:T(8,128)S(1)}, f32[640,4,96]{0,2,1:T(8,128)}, u32[]{:S(2)}) copy-start(f32[640,4,96]{0,2,1:T(8,128)} %get-tuple-element.29) | copy-start | bytes 2949124
  261.1 9.3 %all-to-all-start.1 = ((f32[8,1,960]{2,1,0:T(1,128)}), f32[8,1,960]{2,1,0:T(1,128)S(1)}, u32[]{:S(2)}, u32[]{:S(2)}) async-start(f32[8,1,960]{2,1,0:T(1,128)} %reshape.314), calls=%async_computation.1 | async-start | bytes 65536 | tf_op jit(solution)/shard_map/all_to_all | solution.py:209
  270.4 41.2 %all-to-all-start.3 = ((f32[2,960,384]{2,0,1:T(2,128)}), f32[2,960,384]{2,0,1:T(2,128)}, u32[]{:S(2)}, u32[]{:S(2)}) async-start(f32[2,960,384]{2,0,1:T(2,128)} %copy.96), calls=%async_computation.3 | async-start | bytes 5898240 | tf_op jit(solution)/shard_map/all_to_all | solution.py:207
  275.2 163.8 %reduce-scatter.4.cloned.1.call-start = ((), (), s32[]{:S(2)}) async-start(), calls=%async_computation.7 | async-start | bytes 8355840
  275.6 5.7 %copy-start.5 = (pred[640,640]{0,1:T(8,128)(4,1)}, pred[640,640]{0,1:T(8,128)(4,1)S(1)}, u32[]{:S(2)}) copy-start(pred[640,640]{0,1:T(8,128)(4,1)S(1)} %fusion.21) | copy-start | bytes 1228804
  277.1 2.7 copy-start.2
  323.3 9.8 %copy-start.6 = (pred[640,640]{0,1:T(8,128)(4,1)S(1)}, pred[640,640]{0,1:T(8,128)(4,1)}, u32[]{:S(2)}) copy-start(pred[640,640]{0,1:T(8,128)(4,1)} %copy-done.5) | copy-start | bytes 1228804
  328.2 10.2 %slice-start = ((s8[4718592]{0:T(1024)(128)(4,1)}), s8[524288]{0:T(1024)(128)(4,1)S(1)}, s32[]{:S(2)}) async-start(s8[4718592]{0:T(1024)(128)(4,1)} %bitcast.72), calls=%async_computation.8 | async-start | bytes 1048576
  333.1 5.3 %slice-start.1 = ((s8[4718592]{0:T(1024)(128)(4,1)}), s8[4194304]{0:T(1024)(128)(4,1)S(1)}, s32[]{:S(2)}) async-start(s8[4718592]{0:T(1024)(128)(4,1)} %bitcast.72), calls=%async_computation.9 | async-start | bytes 8388608
  355.3 0.7 copy-start.7
  355.3 85.0 %copy-start.4 = (bf16[640,384]{1,0:T(8,128)(2,1)S(1)}, bf16[640,384]{1,0:T(8,128)(2,1)}, u32[]{:S(2)}) copy-start(bf16[640,384]{1,0:T(8,128)(2,1)} %param.12) | copy-start | bytes 1474564
Sparse Core Ops, SparseCore 0:
  9.5 78.2 all-gather.2
  89.5 73.2 all-gather.4
  355.5 83.5 reduce-scatter.3
